TPU v7x, 256 devices: a whole 4x4x8 slice. The times are simulated.
256 devices in a mesh: section: 8 (over y, core), dp: 32 (over z, x).
Axes of the slice: x: 4, y: 4, z: 8, core: 2. Of those that a mesh axis runs over, the one named last changes fastest.
Arguments:
- hidden_in: bfloat16 [4, 1024, 8192], P(None, 'dp'), may hold values from -6 to 6
- cotangent: bfloat16 [4, 1024, 8192], P(None, 'dp'), may hold values from -6 to 6
- adapter_in: bfloat16 [8, 8192, 128], P('section', 'dp'), may hold values from -0.0625 to 0.0625
- adapter_out: bfloat16 [8, 128, 8192], P('section', None, 'dp'), may hold values from -0.5 to 0.5
- norm_gain: bfloat16 [8, 8192], P('section', 'dp'), may hold values from 0.5 to 1.5
- user_of_row: int32 [4, 1024], P(None, 'dp'), may hold values from 0 to 63, as said below
- included: int32 [4, 64], P(None, 'dp'), may hold values 0 or 1
Outputs:
- grad_in: float32 [8, 8192, 128], P('section', 'dp')
- grad_out: float32 [8, 128, 8192], P('section', None, 'dp')
- user_weights: float32 [4, 64], P(None, 'dp')
Inputs may be any that keep to these rules, and one draw needn't show every extreme that they name: `user_of_row`: within one micro-batch, the rows of the j-th block of 32 rows belong to users j * 2 to j * 2 + 1, in rising order, each of them with one row or more.
All inputs are finite; a program needn't handle non-finite values. No bound on the sum of `included` on one device may be relied on, other than what follows from the above.
Results may differ from a plain program's by a relative error of at most 0.018.
Values may be sent and summed in bfloat16 or wider, within the bound.
A program may use at most 64 MiB of HBM per device.

v0:
```python
import math
import jax
import jax.numpy as jnp
from jax import lax
from jax.sharding import Mesh
from jax.sharding import PartitionSpec as P

F32 = jnp.float32
BF = jnp.bfloat16


def mm(a, b, ca, cb):
    return lax.dot_general(a, b, (((ca,), (cb,)), ((), ())), preferred_element_type=F32)


def swap_route(n, m):
    return [(i * m + j, j * m + i) for i in range(n) for j in range(m)]


def recurrence(z0, y0, c0, norm0, gram, width):
    layers, rows, rank = z0.shape
    z = [z0[l] for l in range(layers)]
    y = [y0[l] for l in range(layers)]
    c = [c0[l] for l in range(layers)]
    square = norm0
    lows, rinvs, fulls, seen = ([], [], [], [])
    for l in range(layers):
        rinv = lax.rsqrt(square / width + 1e-05)
        full = z[l] * rinv
        low = full.astype(BF)
        seen.append(list(y))
        for j in range(layers):
            both = mm(low, gram[l, j], 1, 0)
            z[j] = z[j] + both[:, :rank]
            y[j] = y[j] + both[:, rank:]
        square = square + jnp.sum(low.astype(F32) * (seen[l][l] + y[l]), -1, keepdims=True)
        lows.append(low)
        rinvs.append(rinv)
        fulls.append(full)
    errs, cors = ([None] * layers, [None] * layers)
    for l in range(layers - 1, -1, -1):
        err = c[l].astype(BF)
        mean = jnp.sum(err.astype(F32) * fulls[l], -1, keepdims=True) / width
        cor = rinvs[l] * rinvs[l] * mean
        for j in range(l):
            c[j] = c[j] + rinvs[l] * mm(err, gram[j, l][:, :rank], 1, 1) - cor * seen[l][j]
        errs[l] = err
        cors[l] = cor
    return (lows, errs, rinvs, cors)


def shards(hidden_in, cotangent, adapter_in, adapter_out, norm_gain, user_of_row, included):
    n_s, n_z, n_x = (lax.axis_size(a) for a in ("section", "z", "x"))
    s, zi, xi = (lax.axis_index(a) for a in ("section", "z", "x"))
    plane = ("section", "x")
    layers = n_s
    micro, rows, width = hidden_in.shape
    cols, rank = adapter_in.shape[1:]
    users = included.shape[1]
    dev_rows = micro * rows
    group_rows = dev_rows * n_x
    own_rows = group_rows // (n_s * n_x)
    gain = norm_gain[0]
    a = adapter_in[0]
    bt = adapter_out[0].T
    g = (a.astype(F32) * gain.astype(F32)[:, None]).astype(BF)
    w = jnp.concatenate([jnp.concatenate([g, bt], 1), jnp.broadcast_to(gain[None], (16, cols))], 0)
    w = lax.ppermute(w, ("section", "z"), swap_route(n_s, n_z))
    w = lax.all_gather(w, "z")
    gains = w[:, cols].astype(F32)
    w = w[:, :cols]
    base = (zi * n_x + xi) * users
    key = (user_of_row - base + users * jnp.arange(micro, dtype=jnp.int32)[:, None]).reshape(
        dev_rows
    )
    onehot = (user_of_row - base)[:, :, None] == jnp.arange(users, dtype=jnp.int32)
    inc = jnp.sum(jnp.where(onehot, included[:, None, :], 0), -1).reshape(dev_rows)
    info = jnp.stack([key, inc]).astype(BF)
    info_all = lax.all_gather(info, "x")
    span = n_x * cols
    both = jnp.concatenate(
        [hidden_in.reshape(dev_rows, width), cotangent.reshape(dev_rows, width)], 0
    )
    both = lax.dynamic_slice_in_dim(both, s * span, span, 1)
    both = jnp.moveaxis(both.reshape(2 * dev_rows, n_x, cols), 1, 0)
    both = lax.all_to_all(both, "x", 0, 0, tiled=True)
    x = both[:, :dev_rows].reshape(group_rows, cols)
    cot = both[:, dev_rows:].reshape(group_rows, cols)
    own = lax.dynamic_index_in_dim(w, zi, 0, keepdims=False)[:, rank:]
    zy = jnp.stack([mm(x, w[l], 1, 0) for l in range(layers)])
    ct = jnp.stack([mm(cot, w[l][:, rank:], 1, 0) for l in range(layers)])
    proj = jnp.concatenate([zy, ct], -1).astype(BF)
    gram = jnp.stack([mm(own, w[l], 0, 0) for l in range(layers)]).astype(BF)
    n_plane = n_s * n_x
    proj = jnp.moveaxis(proj.reshape(layers, n_plane, own_rows, 3 * rank), 1, 0)
    gram = gram.reshape(n_plane, rank // n_x, 2 * rank)
    xf = x.astype(F32)
    norm0 = jnp.sum(xf * xf, -1).reshape(n_plane, own_rows, 1)
    proj = jnp.sum(lax.all_to_all(proj, plane, 0, 0, tiled=True).astype(F32), 0)
    gram = jnp.sum(lax.all_to_all(gram, plane, 0, 0, tiled=True).astype(F32), 0).astype(BF)
    norm0 = jnp.sum(lax.all_to_all(norm0, plane, 0, 0, tiled=True), 0)
    gram = lax.all_gather(gram, ("z", "section", "x"))
    gram = gram.reshape(layers, layers, rank, 2 * rank)
    lows, errs, rinvs, cors = recurrence(
        proj[..., :rank], proj[..., rank : 2 * rank], proj[..., 2 * rank :], norm0, gram, width
    )
    pack = jnp.stack(lows + errs)
    scal = jnp.concatenate(rinvs + cors, 1)
    pack = lax.all_gather(pack, plane, axis=1, tiled=True)
    scal = lax.all_gather(scal, plane, axis=0, tiled=True)
    low, err = (pack[:layers], pack[layers:])
    h = x.astype(F32)
    normed = []
    hs = []
    for l in range(layers):
        hs.append(h.astype(BF))
        normed.append((h * scal[:, l : l + 1] * gains[l][None]).astype(BF))
        h = h + mm(low[l], w[l][:, rank:], 1, 1)
    delta = cot.astype(F32)
    deltas = [None] * layers
    for l in range(layers - 1, -1, -1):
        deltas[l] = delta.astype(BF)
        delta = (
            delta
            + scal[:, l : l + 1] * mm(err[l], w[l][:, :rank], 1, 1)
            - scal[:, layers + l : layers + l + 1] * hs[l].astype(F32)
        )
    totals = []
    for i in range(n_x):
        at = slice(i * dev_rows, (i + 1) * dev_rows)
        keys = info_all[i, 0]
        same = keys[:, None] == keys[None, :]
        pairs = 0.0
        for l in range(layers):
            n, e, lo, d = (normed[l][at], err[l][at], low[l][at], deltas[l][at])
            pairs = pairs + mm(n, n, 1, 1) * mm(e, e, 1, 1) + mm(lo, lo, 1, 1) * mm(d, d, 1, 1)
        rowsum = jnp.sum(jnp.where(same, pairs, 0.0), -1)
        totals.append(jnp.sum(jnp.where(same, rowsum[None, :], 0.0), -1))
    totals = lax.psum(jnp.stack(totals), plane)
    bound = 0.8 * math.sqrt(layers * (rows // users) * width * width)
    row_w = info_all[:, 1].astype(F32) * (bound / jnp.maximum(jnp.sqrt(totals), bound))
    mine = lax.dynamic_index_in_dim(row_w, xi, 0, keepdims=False).reshape(micro, rows)
    user_weights = jnp.max(jnp.where(onehot, mine[:, :, None], 0.0), 1)
    row_w = row_w.reshape(group_rows, 1)
    grads = []
    for l in range(layers):
        we = (row_w * err[l].astype(F32)).astype(BF)
        wl = (row_w * low[l].astype(F32)).astype(BF)
        grads.append(jnp.concatenate([mm(normed[l], we, 0, 0), mm(deltas[l], wl, 0, 0)], 1))
    grads = jnp.stack(grads).astype(BF)
    grads = jnp.sum(lax.all_to_all(grads, "z", 0, 0, tiled=True).astype(F32), 0)
    grads = lax.ppermute(grads, ("section", "z"), swap_route(n_s, n_z))
    return (grads[None, :, :rank], grads[:, rank:].T[None], user_weights)


def solution(mesh):
    torus = Mesh(mesh.devices.reshape(mesh.shape["section"], 8, 4), ("section", "z", "x"))
    dp = ("z", "x")
    return jax.shard_map(
        shards,
        mesh=torus,
        in_specs=(
            P(None, dp, None),
            P(None, dp, None),
            P("section", dp, None),
            P("section", None, dp),
            P("section", dp),
            P(None, dp),
            P(None, dp),
        ),
        out_specs=(P("section", dp, None), P("section", None, dp), P(None, dp)),
        check_vma=False,
    )
```

profile of v0, /device:TPU:25, one launch (start us, length us, event | category | flops | bytes accessed | tf_op | source)
XLA Modules:
  0.0 460.0 jit_solution(16412173527792185459)
XLA Ops:
  7.2 0.9 copy.62
  8.2 0.7 reduce.3
  8.9 0.9 fusion.218
  9.9 7.7 %collective-permute-start = (bf16[272,256]{1,0:T(8,128)(2,1)S(1)}, bf16[272,256]{1,0:T(8,128)(2,1)S(1)}, u32[]{:S(2)}, u32[]{:S(2)}) collective-permute-start(bf16[272,256]{1,0:T(8,128)(2,1)S(1)} %pad_maximum_fusion), channel_id=1, source_target_pairs={{0,0},{4,32},{8,64},{12,96},{16,128},{20,160},{24,192},{28,224},{3... | collective-permute-start | bytes 417800 | tf_op jit(solution)/shard_map/ppermute | solution.py:68
  17.6 10.1 %collective-permute-done = bf16[272,256]{1,0:T(8,128)(2,1)S(1)} collective-permute-done((bf16[272,256]{1,0:T(8,128)(2,1)S(1)}, bf16[272,256]{1,0:T(8,128)(2,1)S(1)}, u32[]{:S(2)}, u32[]{:S(2)}) %collective-permute-start) | collective-permute-done | bytes 139296 | tf_op jit(solution)/shard_map/ppermute | solution.py:68
  27.7 0.7 copy-done.50
  28.4 33.7 %all-gather.8.cloned.1.call-done = bf16[2176,256]{1,0:T(8,128)(2,1)} async-done(((bf16[272,256]{1,0:T(8,128)(2,1)}), bf16[2176,256]{1,0:T(8,128)(2,1)}) %all-gather.8.cloned.1.call-update) | async-done | bytes 1114128 | tf_op jit(solution)/shard_map/all_gather | solution.py:69
  62.2 1.4 slice.2149
  65.3 0.8 copy-done.44
  66.1 12.5 %all-to-all-start.3 = ((bf16[32,32,256]{2,1,0:T(8,128)(2,1)}), bf16[32,32,256]{2,1,0:T(8,128)(2,1)}, u32[]{:S(2)}, u32[]{:S(2)}) async-start(bf16[32,32,256]{2,1,0:T(8,128)(2,1)} %bitcast.1095), calls=%async_computation.3 | async-start | bytes 1048576 | tf_op jit(solution)/shard_map/all_to_all | solution.py:100
  78.6 1.8 fusion.201
  80.4 2.0 copy.59
  82.4 5.8 %all-to-all-done.3 = bf16[32,32,256]{2,1,0:T(8,128)(2,1)} async-done(((bf16[32,32,256]{2,1,0:T(8,128)(2,1)}), bf16[32,32,256]{2,1,0:T(8,128)(2,1)}, u32[]{:S(2)}, u32[]{:S(2)}) %all-to-all-start.3) | async-done | bytes 524320 | tf_op jit(solution)/shard_map/all_to_all | solution.py:100
  88.3 3.5 all-to-all-start
  91.8 1.7 reduce_sum.273
  93.6 7.3 %all-to-all-done = bf16[4,256,256]{1,2,0:T(8,128)(2,1)S(1)} async-done(((bf16[4,256,256]{1,2,0:T(8,128)(2,1)}), bf16[4,256,256]{1,2,0:T(8,128)(2,1)S(1)}, u32[]{:S(2)}, u32[]{:S(2)}) %all-to-all-start) | async-done | bytes 524320 | tf_op jit(solution)/shard_map/all_to_all | solution.py:86
  101.0 0.7 reshape.982
  101.7 6.6 %all-to-all-start.1 = ((f32[32,16,1]{1,2,0:T(1,128)}), f32[32,16,1]{1,2,0:T(1,128)S(1)}, u32[]{:S(2)}, u32[]{:S(2)}) async-start(f32[32,16,1]{1,2,0:T(1,128)} %bitcast.4), calls=%async_computation.1 | async-start | bytes 32768 | tf_op jit(solution)/shard_map/all_to_all | solution.py:101
  113.2 2.2 copy.64
  115.4 7.4 %all-to-all-start.2 = ((bf16[32,8,16,384]{3,2,1,0:T(8,128)(2,1)}), bf16[32,8,16,384]{3,2,1,0:T(8,128)(2,1)}, u32[]{:S(2)}, u32[]{:S(2)}) async-start(bf16[32,8,16,384]{3,2,1,0:T(8,128)(2,1)} %copy.64), calls=%async_computation.2 | async-start | bytes 6291456 | tf_op jit(solution)/shard_map/all_to_all | solution.py:99
  123.0 38.1 %all-to-all-done.2 = bf16[32,8,16,384]{3,2,1,0:T(8,128)(2,1)} async-done(((bf16[32,8,16,384]{3,2,1,0:T(8,128)(2,1)}), bf16[32,8,16,384]{3,2,1,0:T(8,128)(2,1)}, u32[]{:S(2)}, u32[]{:S(2)}) %all-to-all-start.2) | async-done | bytes 3145760 | tf_op jit(solution)/shard_map/all_to_all | solution.py:99
  161.1 2.3 convert_reduce_fusion
  163.5 50.2 %all-gather.10.cloned.1.call-done = bf16[8192,256]{1,0:T(8,128)(2,1)} async-done(((bf16[32,256]{1,0:T(8,128)(2,1)}), bf16[8192,256]{1,0:T(8,128)(2,1)}) %all-gather.10.cloned.1.call-update) | async-done | bytes 4194320 | tf_op jit(solution)/shard_map/all_gather | solution.py:102
  213.7 1.5 slice_bitcast_fusion.99
  215.2 1.2 fusion.503
  216.4 1.0 fusion.501
  217.7 1.0 fusion.515
  218.7 1.0 fusion.516
  219.7 1.0 fusion.499
  221.0 1.0 fusion.517
  222.0 1.0 fusion.519
  222.9 1.0 fusion.518
  223.9 1.0 fusion.497
  225.2 1.0 fusion.520
  226.2 1.0 fusion.523
  227.2 1.0 fusion.522
  228.1 1.0 fusion.521
  229.1 1.0 fusion.495
  230.5 1.0 fusion.524
  242.6 0.6 copy-done.51
  243.6 6.6 %all_gather.27 = bf16[4,2,128]{2,1,0:T(2,128)(2,1)S(1)} all-gather(bf16[1,2,128]{2,1,0:T(2,128)(2,1)S(1)} %pad_maximum_fusion.2), channel_id=1, replica_groups=mesh['section'=8,'z'=8,'x'=4] {'x'}, dimensions={0}, use_global_device_ids=true | all-gather | bytes 2560 | tf_op jit(solution)/shard_map/all_gather | solution.py:79
  250.1 0.6 slice.2329
  250.7 0.6 slice_bitcast_fusion.269
  251.9 45.5 %all_gather.26 = f32[512,16]{1,0:T(8,128)S(1)} all-gather(f32[16,16]{1,0:T(8,128)S(1)} %copy.65), channel_id=1, replica_groups=mesh['section'=8,'z'=8,'x'=4] {'section','x'}, dimensions={0}, use_global_device_ids=true | all-gather | bytes 33792 | tf_op jit(solution)/shard_map/all_gather | solution.py:110
  297.4 2.6 slice_reduce_fusion.14
  300.1 0.8 copy.66
  301.1 0.8 fusion.276
  301.9 0.8 fusion.299
  302.7 0.8 fusion.322
  303.7 1.5 multiply_convert_fusion.6
  305.5 1.2 multiply_convert_fusion.5
  307.1 1.1 multiply_convert_fusion.4
  315.3 0.3 copy-done.33
  332.2 55.6 %psum.7 = f32[4,128]{1,0:T(4,128)S(1)} all-reduce(f32[4,128]{1,0:T(4,128)S(1)} %pad_maximum_fusion.1), channel_id=1, replica_groups=mesh['section'=8,'z'=8,'x'=4] {'section','x'}, use_global_device_ids=true, to_apply=%region_28.29 | all-reduce | flops 512 | bytes 4096 | tf_op jit(solution)/shard_map/psum | solution.py:139
  388.2 1.3 convolution_convert_fusion.31
  389.5 1.3 convolution_convert_fusion.28
  391.2 1.3 convolution_convert_fusion.26
  392.5 1.3 convolution_convert_fusion.27
  397.4 30.1 %all_to_all.25 = bf16[8,256,256]{1,2,0:T(8,128)(2,1)S(1)} all-to-all(bf16[8,256,256]{1,2,0:T(8,128)(2,1)S(1)} %fusion.217), channel_id=1, replica_groups=mesh['section'=8,'z'=8,'x'=4] {'z'}, dimensions={0} | all-to-all | bytes 2097152 | tf_op jit(solution)/shard_map/all_to_all | solution.py:151
  427.7 8.4 %collective-permute-start.1 = (f32[256,256]{0,1:T(8,128)S(1)}, f32[256,256]{0,1:T(8,128)S(1)}, u32[]{:S(2)}, u32[]{:S(2)}) collective-permute-start(f32[256,256]{0,1:T(8,128)S(1)} %convert_reduce_fusion.1), channel_id=1, source_target_pairs={{0,0},{4,32},{8,64},{12,96},{16,128},{20,160},{24,192},{28,224},{3... | collective-permute-start | bytes 786440 | tf_op jit(solution)/shard_map/ppermute | solution.py:152
  436.2 0.7 select_reduce_fusion
  436.9 15.1 %collective-permute-done.1 = f32[256,256]{0,1:T(8,128)S(1)} collective-permute-done((f32[256,256]{0,1:T(8,128)S(1)}, f32[256,256]{0,1:T(8,128)S(1)}, u32[]{:S(2)}, u32[]{:S(2)}) %collective-permute-start.1) | collective-permute-done | bytes 262176 | tf_op jit(solution)/shard_map/ppermute | solution.py:152
  452.0 0.7 slice_bitcast_fusion
  452.7 0.8 copy.70
  (481 shorter events, 48.1 us)
Async XLA Ops:
  7.2 55.0 %all-gather.8.cloned.1.call-start = ((), (), s32[]{:S(2)}) async-start(), calls=%async_computation.6 | async-start | bytes 1253376 | tf_op jit(solution)/shard_map/all_gather | solution.py:69
  9.9 17.9 %collective-permute-start = (bf16[272,256]{1,0:T(8,128)(2,1)S(1)}, bf16[272,256]{1,0:T(8,128)(2,1)S(1)}, u32[]{:S(2)}, u32[]{:S(2)}) collective-permute-start(bf16[272,256]{1,0:T(8,128)(2,1)S(1)} %pad_maximum_fusion), channel_id=1, source_target_pairs={{0,0},{4,32},{8,64},{12,96},{16,128},{20,160},{24,192},{28,224},{3... | collective-permute-start | bytes 417800 | tf_op jit(solution)/shard_map/ppermute | solution.py:68
  63.5 15.0 %copy-start.6 = (bf16[4,32,8192]{2,1,0:T(8,128)(2,1)S(1)}, bf16[4,32,8192]{2,1,0:T(8,128)(2,1)}, u32[]{:S(2)}) copy-start(bf16[4,32,8192]{2,1,0:T(8,128)(2,1)} %param.7) | copy-start | bytes 6291460
  66.1 22.2 %all-to-all-start.3 = ((bf16[32,32,256]{2,1,0:T(8,128)(2,1)}), bf16[32,32,256]{2,1,0:T(8,128)(2,1)}, u32[]{:S(2)}, u32[]{:S(2)}) async-start(bf16[32,32,256]{2,1,0:T(8,128)(2,1)} %bitcast.1095), calls=%async_computation.3 | async-start | bytes 1048576 | tf_op jit(solution)/shard_map/all_to_all | solution.py:100
  88.3 12.6 %all-to-all-start = ((bf16[4,256,256]{1,2,0:T(8,128)(2,1)}), bf16[4,256,256]{1,2,0:T(8,128)(2,1)S(1)}, u32[]{:S(2)}, u32[]{:S(2)}) async-start(bf16[4,256,256]{1,2,0:T(8,128)(2,1)} %bitcast.3), calls=%async_computation | async-start | bytes 1048576 | tf_op jit(solution)/shard_map/all_to_all | solution.py:86
  91.8 122.0 %all-gather.10.cloned.1.call-start = ((), (), s32[]{:S(2)}) async-start(), calls=%async_computation.7 | async-start | bytes 4210688 | tf_op jit(solution)/shard_map/all_gather | solution.py:102
  100.9 199.1 %copy-start.3 = (bf16[4,256,256]{1,2,0:T(8,128)(2,1)}, bf16[4,256,256]{1,2,0:T(8,128)(2,1)S(1)}, u32[]{:S(2)}) copy-start(bf16[4,256,256]{1,2,0:T(8,128)(2,1)S(1)} %all-to-all-done) | copy-start | bytes 1572868
  101.7 13.7 %all-to-all-start.1 = ((f32[32,16,1]{1,2,0:T(1,128)}), f32[32,16,1]{1,2,0:T(1,128)S(1)}, u32[]{:S(2)}, u32[]{:S(2)}) async-start(f32[32,16,1]{1,2,0:T(1,128)} %bitcast.4), calls=%async_computation.1 | async-start | bytes 32768 | tf_op jit(solution)/shard_map/all_to_all | solution.py:101
  108.9 2.3 copy-start.30
  108.9 2.3 copy-start.32
  108.9 2.3 copy-start.34
  108.9 2.3 copy-start.36
  108.9 2.3 copy-start.38
  108.9 2.3 copy-start.40
  108.9 2.3 copy-start.42
  108.9 2.3 copy-start.45
  115.4 45.6 %all-to-all-start.2 = ((bf16[32,8,16,384]{3,2,1,0:T(8,128)(2,1)}), bf16[32,8,16,384]{3,2,1,0:T(8,128)(2,1)}, u32[]{:S(2)}, u32[]{:S(2)}) async-start(bf16[32,8,16,384]{3,2,1,0:T(8,128)(2,1)} %copy.64), calls=%async_computation.2 | async-start | bytes 6291456 | tf_op jit(solution)/shard_map/all_to_all | solution.py:99
  122.8 180.8 %all-gather.6.cloned.1.call-start = ((), (), s32[]{:S(2)}) async-start(), calls=%async_computation.5 | async-start | bytes 2162688 | tf_op jit(solution)/shard_map/all_gather | solution.py:109
  213.7 17.7 %copy-start.2 = (bf16[8192,256]{1,0:T(8,128)(2,1)S(1)}, bf16[8192,256]{1,0:T(8,128)(2,1)}, u32[]{:S(2)}) copy-start(bf16[8192,256]{1,0:T(8,128)(2,1)} %all-gather.10.cloned.1.call-done) | copy-start | bytes 12582916
  235.7 7.5 %copy-start.72 = (s32[4,32]{1,0:T(4,128)S(1)}, s32[4,32]{1,0:T(4,128)}, u32[]{:S(2)}) copy-start(s32[4,32]{1,0:T(4,128)} %param.12) | copy-start | bytes 1540
  235.7 7.6 %copy-start.73 = (s32[4,2]{0,1:T(2,128)S(1)}, s32[4,2]{0,1:T(2,128)}, u32[]{:S(2)}) copy-start(s32[4,2]{0,1:T(2,128)} %param.13) | copy-start | bytes 100
  251.5 52.1 %copy-start.5 = (f32[4,128,256]{2,1,0:T(8,128)}, f32[4,128,256]{2,1,0:T(8,128)S(1)}, u32[]{:S(2)}) copy-start(f32[4,128,256]{2,1,0:T(8,128)S(1)} %copy.68) | copy-start | bytes 1572868
  300.0 7.1 %copy-start.52 = (f32[512]{0:T(512)}, f32[512]{0:T(512)S(1)}, u32[]{:S(2)}) copy-start(f32[512]{0:T(512)S(1)} %get-tuple-element.15) | copy-start | bytes 6148
  300.0 8.5 %copy-start.54 = (f32[512]{0:T(512)}, f32[512]{0:T(512)S(1)}, u32[]{:S(2)}) copy-start(f32[512]{0:T(512)S(1)} %get-tuple-element.17) | copy-start | bytes 6148
  300.0 9.1 %copy-start.56 = (f32[512]{0:T(512)}, f32[512]{0:T(512)S(1)}, u32[]{:S(2)}) copy-start(f32[512]{0:T(512)S(1)} %get-tuple-element.19) | copy-start | bytes 6148
  300.0 9.7 %copy-start.58 = (f32[512]{0:T(512)}, f32[512]{0:T(512)S(1)}, u32[]{:S(2)}) copy-start(f32[512]{0:T(512)S(1)} %get-tuple-element.21) | copy-start | bytes 6148
  300.0 3.7 copy-start.46
  303.7 3.4 copy-start.1
  305.2 6.9 %copy-start.13 = (bf16[512,256]{1,0:T(8,128)(2,1)}, bf16[512,256]{1,0:T(8,128)(2,1)S(1)}, u32[]{:S(2)}) copy-start(bf16[512,256]{1,0:T(8,128)(2,1)S(1)} %get-tuple-element.175) | copy-start | bytes 786436
  305.2 3.3 copy-start.35
  306.7 5.6 %copy-start.17 = (bf16[512,256]{1,0:T(8,128)(2,1)}, bf16[512,256]{1,0:T(8,128)(2,1)S(1)}, u32[]{:S(2)}) copy-start(bf16[512,256]{1,0:T(8,128)(2,1)S(1)} %get-tuple-element.179) | copy-start | bytes 786436
  306.7 2.4 copy-start.37
  308.2 4.3 copy-start.15
  308.8 3.9 copy-start.11
  309.4 3.4 copy-start.9
  310.0 3.7 copy-start.7
  310.0 3.5 copy-start.49
  310.0 3.7 copy-start.43
  310.0 3.7 copy-start.61
  310.6 3.7 copy-start.18
  310.6 3.4 copy-start.59
  310.6 3.4 copy-start.67
  314.0 17.4 %copy-start.20 = (bf16[512,256]{1,0:T(8,128)(2,1)}, bf16[512,256]{1,0:T(8,128)(2,1)S(1)}, u32[]{:S(2)}) copy-start(bf16[512,256]{1,0:T(8,128)(2,1)S(1)} %get-tuple-element.197) | copy-start | bytes 786436
  314.3 16.6 %copy-start.22 = (bf16[512,256]{1,0:T(8,128)(2,1)}, bf16[512,256]{1,0:T(8,128)(2,1)S(1)}, u32[]{:S(2)}) copy-start(bf16[512,256]{1,0:T(8,128)(2,1)S(1)} %get-tuple-element.193) | copy-start | bytes 786436
  314.6 15.8 %copy-start.24 = (bf16[512,256]{1,0:T(8,128)(2,1)}, bf16[512,256]{1,0:T(8,128)(2,1)S(1)}, u32[]{:S(2)}) copy-start(bf16[512,256]{1,0:T(8,128)(2,1)S(1)} %get-tuple-element.189) | copy-start | bytes 786436
  315.0 14.9 %copy-start.26 = (bf16[512,256]{1,0:T(8,128)(2,1)}, bf16[512,256]{1,0:T(8,128)(2,1)S(1)}, u32[]{:S(2)}) copy-start(bf16[512,256]{1,0:T(8,128)(2,1)S(1)} %get-tuple-element.185) | copy-start | bytes 786436
  315.3 14.1 %copy-start.28 = (bf16[512,256]{1,0:T(8,128)(2,1)}, bf16[512,256]{1,0:T(8,128)(2,1)S(1)}, u32[]{:S(2)}) copy-start(bf16[512,256]{1,0:T(8,128)(2,1)S(1)} %get-tuple-element.181) | copy-start | bytes 786436
  315.9 13.0 %copy-start.29 = (bf16[512,256]{1,0:T(8,128)(2,1)}, bf16[512,256]{1,0:T(8,128)(2,1)S(1)}, u32[]{:S(2)}) copy-start(bf16[512,256]{1,0:T(8,128)(2,1)S(1)} %get-tuple-element.177) | copy-start | bytes 786436
  316.2 3.4 copy-start.4
  316.3 3.4 copy-start.71
  316.6 3.6 copy-start.48
  320.3 3.4 copy-start.70
  320.6 3.6 copy-start.47
  324.4 3.4 copy-start.69
  328.4 3.5 copy-start.68
  328.6 59.2 %copy-start.62 = (bf16[4,1,128]{2,1,0:T(2,128)(2,1)S(1)}, bf16[4,1,128]{2,1,0:T(2,128)(2,1)}, u32[]{:S(2)}) copy-start(bf16[4,1,128]{2,1,0:T(2,128)(2,1)} %slice.2329) | copy-start | bytes 3076
  330.2 60.6 %copy-start.14 = (bf16[512,256]{1,0:T(8,128)(2,1)S(1)}, bf16[512,256]{1,0:T(8,128)(2,1)}, u32[]{:S(2)}) copy-start(bf16[512,256]{1,0:T(8,128)(2,1)} %copy-done.13) | copy-start | bytes 786436
  332.1 61.8 %copy-start.27 = (bf16[512,256]{1,0:T(8,128)(2,1)S(1)}, bf16[512,256]{1,0:T(8,128)(2,1)}, u32[]{:S(2)}) copy-start(bf16[512,256]{1,0:T(8,128)(2,1)} %copy-done.26) | copy-start | bytes 786436
  388.1 6.1 %copy-start.16 = (bf16[512,256]{1,0:T(8,128)(2,1)S(1)}, bf16[512,256]{1,0:T(8,128)(2,1)}, u32[]{:S(2)}) copy-start(bf16[512,256]{1,0:T(8,128)(2,1)} %copy-done.15) | copy-start | bytes 786436
  389.5 5.1 %copy-start.25 = (bf16[512,256]{1,0:T(8,128)(2,1)S(1)}, bf16[512,256]{1,0:T(8,128)(2,1)}, u32[]{:S(2)}) copy-start(bf16[512,256]{1,0:T(8,128)(2,1)} %copy-done.24) | copy-start | bytes 786436
  390.8 4.1 copy-start.12
  391.2 4.1 copy-start.23
  392.5 3.1 copy-start.10
  427.7 24.3 %collective-permute-start.1 = (f32[256,256]{0,1:T(8,128)S(1)}, f32[256,256]{0,1:T(8,128)S(1)}, u32[]{:S(2)}, u32[]{:S(2)}) collective-permute-start(f32[256,256]{0,1:T(8,128)S(1)} %convert_reduce_fusion.1), channel_id=1, source_target_pairs={{0,0},{4,32},{8,64},{12,96},{16,128},{20,160},{24,192},{28,224},{3... | collective-permute-start | bytes 786440 | tf_op jit(solution)/shard_map/ppermute | solution.py:152
  (19 other events, 23.0 us)
Sparse Core Ops, SparseCore 0:
  28.5 33.5 all-gather.7
  96.3 117.3 all-gather.9
  243.3 46.5 all-gather.5
where the time goes:
time: 462 us; the launch traced here: 460 us
  waiting for transfers between devices  161 us (35%)
  blocking collectives  138 us (30%)
  matrix products  68.7 us (15%)
  starting transfers between devices  46.2 us (10%)
  local copies, waits for them, and re-layouts  19.8 us (4%)
  between operations  15.9 us (3%)
  other arithmetic  11.1 us (2%)
    dot_general x266, matrix products, mm(): lax.dot_general(a, b, (((ca,), (cb,)), ((), ())), preferred_element_type=...  68.7 us
    psum x1, blocking collectives, shards(): totals = lax.psum(jnp.stack(totals), plane)  55.6 us
    all_gather x1, waiting for transfers between devices, shards(): gram = lax.all_gather(gram, ('z', 'section', 'x'))  50.2 us
    all_gather x1, blocking collectives, shards(): scal = lax.all_gather(scal, plane, axis=0, tiled=True)  45.5 us
    all_to_all x1, waiting for transfers between devices, shards(): proj = jnp.sum(lax.all_to_all(proj, plane, 0, 0, tiled=True).astype(F32), 0)  38.1 us
    all_gather x1, waiting for transfers between devices, shards(): w = lax.all_gather(w, 'z')  33.7 us
    all_to_all x1, blocking collectives, shards(): grads = jnp.sum(lax.all_to_all(grads, 'z', 0, 0, tiled=True).astype(F32), 0)  30.1 us
    ppermute x1, waiting for transfers between devices, shards(): grads = lax.ppermute(grads, ('section', 'z'), swap_route(n_s, n_z))  15.1 us
  transfers between devices with their start and end apart: 9, of which 7 were waited for; matrix products, arithmetic and copies ran while one was open for 5% of the time, Pallas kernels for 0%

commit v1 on v0

--- a/solution.py
+++ b/solution.py
@@ -136,7 +136,9 @@
             pairs = pairs + mm(n, n, 1, 1) * mm(e, e, 1, 1) + mm(lo, lo, 1, 1) * mm(d, d, 1, 1)
         rowsum = jnp.sum(jnp.where(same, pairs, 0.0), -1)
         totals.append(jnp.sum(jnp.where(same, rowsum[None, :], 0.0), -1))
-    totals = lax.psum(jnp.stack(totals), plane)
+    own_2 = jnp.stack(totals)
+    blocks = lax.all_gather(own_2, plane)
+    totals = jnp.sum(blocks, axis=0)
     bound = 0.8 * math.sqrt(layers * (rows // users) * width * width)
     row_w = info_all[:, 1].astype(F32) * (bound / jnp.maximum(jnp.sqrt(totals), bound))
     mine = lax.dynamic_index_in_dim(row_w, xi, 0, keepdims=False).reshape(micro, rows)

time: 462 us -> 470 us (1.017)
  blocking collectives: 138 us -> 93.3 us
  waiting for transfers between devices: 161 us -> 195 us
  other arithmetic: 11.1 us -> 23.6 us
    psum x1 -> x0, blocking collectives: 55.6 us -> none  [shards(): totals = lax.psum(jnp.stack(totals), plane)]
    all_gather x0 -> x1, blocking collectives: none -> 41.3 us  [shards(): blocks = lax.all_gather(own_2, plane)]
    all_to_all x1 -> x0, blocking collectives: 30.1 us -> none  [shards(): grads = jnp.sum(lax.all_to_all(grads, 'z', 0, 0, tiled=True).astype(F32), 0)]
    all_to_all x0 -> x1, waiting for transfers between devices: none -> 29.3 us  [shards(): grads = jnp.sum(lax.all_to_all(grads, 'z', 0, 0, tiled=True).astype(F32), 0)]
    unnamed x15 -> x16, other arithmetic: 1.35 us -> 10 us
    ppermute x1, waiting for transfers between devices: 15.1 us -> 21.6 us  [shards(): grads = lax.ppermute(grads, ('section', 'z'), swap_route(n_s, n_z))]
    ppermute x1, starting transfers between devices: 8.41 us -> 1.92 us  [shards(): grads = lax.ppermute(grads, ('section', 'z'), swap_route(n_s, n_z))]
  transfers between devices with their start and end apart: 9 -> 10, of which waited for: 7 -> 8; matrix products, arithmetic and copies ran while one was open for 5% -> 6% of each run, Pallas kernels for 0% -> 0%
where the time goes in v1:
time: 470 us; the launch traced here: 468 us
  waiting for transfers between devices  195 us (41%)
  blocking collectives  93.3 us (20%)
  matrix products  73.2 us (16%)
  starting transfers between devices  43.6 us (9%)
  other arithmetic  23.6 us (5%)
  local copies, waits for them, and re-layouts  23.2 us (5%)
  between operations  15.8 us (3%)
    dot_general x266, matrix products, mm(): lax.dot_general(a, b, (((ca,), (cb,)), ((), ())), preferred_element_type=...  73.2 us
    all_gather x1, waiting for transfers between devices, shards(): gram = lax.all_gather(gram, ('z', 'section', 'x'))  49.6 us
    all_gather x1, blocking collectives, shards(): scal = lax.all_gather(scal, plane, axis=0, tiled=True)  45.4 us
    all_gather x1, blocking collectives, shards(): blocks = lax.all_gather(own_2, plane)  41.3 us
    all_to_all x1, waiting for transfers between devices, shards(): proj = jnp.sum(lax.all_to_all(proj, plane, 0, 0, tiled=True).astype(F32), 0)  37.6 us
    all_gather x1, waiting for transfers between devices, shards(): w = lax.all_gather(w, 'z')  33.7 us
    all_to_all x1, waiting for transfers between devices, shards(): grads = jnp.sum(lax.all_to_all(grads, 'z', 0, 0, tiled=True).astype(F32), 0)  29.3 us
    ppermute x1, waiting for transfers between devices, shards(): grads = lax.ppermute(grads, ('section', 'z'), swap_route(n_s, n_z))  21.6 us
  transfers between devices with their start and end apart: 10, of which 8 were waited for; matrix products, arithmetic and copies ran while one was open for 6% of the time, Pallas kernels for 0%

profile of v1, /device:TPU:25, one launch (start us, length us, event | category | flops | bytes accessed | tf_op | source)
XLA Modules:
  0.0 468.0 jit_solution(15670037394526673433)
XLA Ops:
  7.2 0.9 copy.60
  8.2 0.7 reduce.4
  8.9 0.9 fusion.218
  9.9 7.7 %collective-permute-start = (bf16[272,256]{1,0:T(8,128)(2,1)S(1)}, bf16[272,256]{1,0:T(8,128)(2,1)S(1)}, u32[]{:S(2)}, u32[]{:S(2)}) collective-permute-start(bf16[272,256]{1,0:T(8,128)(2,1)S(1)} %pad_maximum_fusion), channel_id=1, source_target_pairs={{0,0},{4,32},{8,64},{12,96},{16,128},{20,160},{24,192},{28,224},{3... | collective-permute-start | bytes 417800 | tf_op jit(solution)/shard_map/ppermute | solution.py:68
  17.6 10.1 %collective-permute-done = bf16[272,256]{1,0:T(8,128)(2,1)S(1)} collective-permute-done((bf16[272,256]{1,0:T(8,128)(2,1)S(1)}, bf16[272,256]{1,0:T(8,128)(2,1)S(1)}, u32[]{:S(2)}, u32[]{:S(2)}) %collective-permute-start) | collective-permute-done | bytes 139296 | tf_op jit(solution)/shard_map/ppermute | solution.py:68
  28.4 33.7 %all-gather.10.cloned.1.call-done = bf16[2176,256]{1,0:T(8,128)(2,1)} async-done(((bf16[272,256]{1,0:T(8,128)(2,1)}), bf16[2176,256]{1,0:T(8,128)(2,1)}) %all-gather.10.cloned.1.call-update) | async-done | bytes 1114128 | tf_op jit(solution)/shard_map/all_gather | solution.py:69
  62.2 1.4 slice.2149
  65.3 0.8 copy-done.34
  66.1 12.5 %all-to-all-start.3 = ((bf16[32,32,256]{2,1,0:T(8,128)(2,1)}), bf16[32,32,256]{2,1,0:T(8,128)(2,1)}, u32[]{:S(2)}, u32[]{:S(2)}) async-start(bf16[32,32,256]{2,1,0:T(8,128)(2,1)} %bitcast.1095), calls=%async_computation.3 | async-start | bytes 1048576 | tf_op jit(solution)/shard_map/all_to_all | solution.py:100
  78.6 1.8 fusion.201
  80.4 2.0 copy.57
  82.5 5.8 %all-to-all-done.3 = bf16[32,32,256]{2,1,0:T(8,128)(2,1)} async-done(((bf16[32,32,256]{2,1,0:T(8,128)(2,1)}), bf16[32,32,256]{2,1,0:T(8,128)(2,1)}, u32[]{:S(2)}, u32[]{:S(2)}) %all-to-all-start.3) | async-done | bytes 524320 | tf_op jit(solution)/shard_map/all_to_all | solution.py:100
  88.3 3.5 all-to-all-start
  91.8 1.7 reduce_sum.282
  93.6 7.3 %all-to-all-done = bf16[4,256,256]{1,2,0:T(8,128)(2,1)S(1)} async-done(((bf16[4,256,256]{1,2,0:T(8,128)(2,1)}), bf16[4,256,256]{1,2,0:T(8,128)(2,1)S(1)}, u32[]{:S(2)}, u32[]{:S(2)}) %all-to-all-start) | async-done | bytes 524320 | tf_op jit(solution)/shard_map/all_to_all | solution.py:86
  101.0 0.7 reshape.1001
  101.7 6.6 %all-to-all-start.1 = ((f32[32,16,1]{1,2,0:T(1,128)}), f32[32,16,1]{1,2,0:T(1,128)S(1)}, u32[]{:S(2)}, u32[]{:S(2)}) async-start(f32[32,16,1]{1,2,0:T(1,128)} %bitcast.4), calls=%async_computation.1 | async-start | bytes 32768 | tf_op jit(solution)/shard_map/all_to_all | solution.py:101
  113.1 2.2 copy.62
  115.4 7.4 %all-to-all-start.2 = ((bf16[32,8,16,384]{3,2,1,0:T(8,128)(2,1)}), bf16[32,8,16,384]{3,2,1,0:T(8,128)(2,1)}, u32[]{:S(2)}, u32[]{:S(2)}) async-start(bf16[32,8,16,384]{3,2,1,0:T(8,128)(2,1)} %copy.62), calls=%async_computation.2 | async-start | bytes 6291456 | tf_op jit(solution)/shard_map/all_to_all | solution.py:99
  123.5 37.6 %all-to-all-done.2 = bf16[32,8,16,384]{3,2,1,0:T(8,128)(2,1)} async-done(((bf16[32,8,16,384]{3,2,1,0:T(8,128)(2,1)}), bf16[32,8,16,384]{3,2,1,0:T(8,128)(2,1)}, u32[]{:S(2)}, u32[]{:S(2)}) %all-to-all-start.2) | async-done | bytes 3145760 | tf_op jit(solution)/shard_map/all_to_all | solution.py:99
  161.1 2.3 convert_reduce_fusion
  164.1 49.6 %all-gather.12.cloned.1.call-done = bf16[8192,256]{1,0:T(8,128)(2,1)} async-done(((bf16[32,256]{1,0:T(8,128)(2,1)}), bf16[8192,256]{1,0:T(8,128)(2,1)}) %all-gather.12.cloned.1.call-update) | async-done | bytes 4194320 | tf_op jit(solution)/shard_map/all_gather | solution.py:102
  213.7 1.5 slice_bitcast_fusion.99
  215.2 1.2 fusion.503
  216.4 1.0 fusion.501
  218.9 1.0 fusion.516
  219.8 1.0 fusion.517
  220.8 1.0 fusion.499
  223.2 1.0 fusion.518
  224.2 1.0 fusion.520
  225.1 1.0 fusion.519
  226.1 1.0 fusion.497
  228.5 1.0 fusion.521
  229.5 1.0 fusion.524
  230.5 1.0 fusion.523
  231.4 1.0 fusion.522
  232.4 1.0 fusion.495
  234.9 1.0 fusion.525
  240.4 0.7 constant_dynamic-update-slice_fusion.8
  249.1 0.8 constant_dynamic-update-slice_fusion.7
  254.4 6.6 %all_gather.33 = bf16[4,2,128]{2,1,0:T(2,128)(2,1)S(1)} all-gather(bf16[1,2,128]{2,1,0:T(2,128)(2,1)S(1)} %pad_maximum_fusion.1), channel_id=1, replica_groups=mesh['section'=8,'z'=8,'x'=4] {'x'}, dimensions={0}, use_global_device_ids=true | all-gather | bytes 2560 | tf_op jit(solution)/shard_map/all_gather | solution.py:79
  262.9 45.4 %all_gather.32 = f32[512,16]{1,0:T(8,128)S(1)} all-gather(f32[16,16]{1,0:T(8,128)S(1)} %copy.63), channel_id=1, replica_groups=mesh['section'=8,'z'=8,'x'=4] {'section','x'}, dimensions={0}, use_global_device_ids=true | all-gather | bytes 33792 | tf_op jit(solution)/shard_map/all_gather | solution.py:110
  308.4 2.6 slice_reduce_fusion.14
  311.0 0.9 copy.64
  312.0 0.8 fusion.276
  312.8 0.8 fusion.299
  313.6 0.8 fusion.322
  314.4 0.8 fusion.352
  315.2 1.3 multiply_convert_fusion.6
  316.9 1.2 multiply_convert_fusion.5
  318.5 1.1 multiply_convert_fusion.4
  343.5 41.3 %all-gather.3 = f32[32,4,128]{2,1,0:T(4,128)S(1)} all-gather(f32[1,4,128]{2,1,0:T(4,128)S(1)} %maximum_bitcast_fusion.9), channel_id=4, replica_groups=mesh['section'=8,'z'=8,'x'=4] {'section','x'}, dimensions={0}, use_global_device_ids=true | all-gather | bytes 67584 | tf_op jit(solution)/shard_map/all_gather | solution.py:140
  384.9 1.3 convolution_convert_fusion.30
  386.2 1.3 convolution_convert_fusion.31
  388.2 1.3 convolution_convert_fusion.28
  389.5 1.3 convolution_convert_fusion.29
  391.5 1.3 convolution_convert_fusion.26
  392.7 1.3 convolution_convert_fusion.27
  394.7 1.3 convolution_convert_fusion.24
  402.3 3.9 all-to-all-start.4
  406.2 29.3 %all-to-all-done.4 = bf16[8,256,256]{1,2,0:T(8,128)(2,1)S(1)} async-done(((bf16[8,256,256]{1,2,0:T(8,128)(2,1)}), bf16[8,256,256]{1,2,0:T(8,128)(2,1)S(1)}, u32[]{:S(2)}, u32[]{:S(2)}) %all-to-all-start.4) | async-done | bytes 1048608 | tf_op jit(solution)/shard_map/all_to_all | solution.py:153
  435.7 1.9 collective-permute-start.1
  438.4 21.6 %collective-permute-done.1 = f32[256,256]{0,1:T(8,128)S(1)} collective-permute-done((f32[256,256]{0,1:T(8,128)S(1)}, f32[256,256]{0,1:T(8,128)S(1)}, u32[]{:S(2)}, u32[]{:S(2)}) %collective-permute-start.1) | collective-permute-done | bytes 262176 | tf_op jit(solution)/shard_map/ppermute | solution.py:154
  460.7 0.8 copy.67
  (496 shorter events, 66.8 us)
Async XLA Ops:
  7.2 55.0 %all-gather.10.cloned.1.call-start = ((), (), s32[]{:S(2)}) async-start(), calls=%async_computation.6 | async-start | bytes 1253376 | tf_op jit(solution)/shard_map/all_gather | solution.py:69
  9.9 17.9 %collective-permute-start = (bf16[272,256]{1,0:T(8,128)(2,1)S(1)}, bf16[272,256]{1,0:T(8,128)(2,1)S(1)}, u32[]{:S(2)}, u32[]{:S(2)}) collective-permute-start(bf16[272,256]{1,0:T(8,128)(2,1)S(1)} %pad_maximum_fusion), channel_id=1, source_target_pairs={{0,0},{4,32},{8,64},{12,96},{16,128},{20,160},{24,192},{28,224},{3... | collective-permute-start | bytes 417800 | tf_op jit(solution)/shard_map/ppermute | solution.py:68
  63.5 15.1 %copy-start.3 = (bf16[4,32,8192]{2,1,0:T(8,128)(2,1)S(1)}, bf16[4,32,8192]{2,1,0:T(8,128)(2,1)}, u32[]{:S(2)}) copy-start(bf16[4,32,8192]{2,1,0:T(8,128)(2,1)} %param.7) | copy-start | bytes 6291460
  66.1 22.2 %all-to-all-start.3 = ((bf16[32,32,256]{2,1,0:T(8,128)(2,1)}), bf16[32,32,256]{2,1,0:T(8,128)(2,1)}, u32[]{:S(2)}, u32[]{:S(2)}) async-start(bf16[32,32,256]{2,1,0:T(8,128)(2,1)} %bitcast.1095), calls=%async_computation.3 | async-start | bytes 1048576 | tf_op jit(solution)/shard_map/all_to_all | solution.py:100
  88.3 12.6 %all-to-all-start = ((bf16[4,256,256]{1,2,0:T(8,128)(2,1)}), bf16[4,256,256]{1,2,0:T(8,128)(2,1)S(1)}, u32[]{:S(2)}, u32[]{:S(2)}) async-start(bf16[4,256,256]{1,2,0:T(8,128)(2,1)} %bitcast.3), calls=%async_computation | async-start | bytes 1048576 | tf_op jit(solution)/shard_map/all_to_all | solution.py:86
  91.8 121.9 %all-gather.12.cloned.1.call-start = ((), (), s32[]{:S(2)}) async-start(), calls=%async_computation.7 | async-start | bytes 4210688 | tf_op jit(solution)/shard_map/all_gather | solution.py:102
  101.7 13.7 %all-to-all-start.1 = ((f32[32,16,1]{1,2,0:T(1,128)}), f32[32,16,1]{1,2,0:T(1,128)S(1)}, u32[]{:S(2)}, u32[]{:S(2)}) async-start(f32[32,16,1]{1,2,0:T(1,128)} %bitcast.4), calls=%async_computation.1 | async-start | bytes 32768 | tf_op jit(solution)/shard_map/all_to_all | solution.py:101
  115.4 45.7 %all-to-all-start.2 = ((bf16[32,8,16,384]{3,2,1,0:T(8,128)(2,1)}), bf16[32,8,16,384]{3,2,1,0:T(8,128)(2,1)}, u32[]{:S(2)}, u32[]{:S(2)}) async-start(bf16[32,8,16,384]{3,2,1,0:T(8,128)(2,1)} %copy.62), calls=%async_computation.2 | async-start | bytes 6291456 | tf_op jit(solution)/shard_map/all_to_all | solution.py:99
  122.8 192.4 %all-gather.8.cloned.1.call-start = ((), (), s32[]{:S(2)}) async-start(), calls=%async_computation.5 | async-start | bytes 2162688 | tf_op jit(solution)/shard_map/all_gather | solution.py:109
  123.4 94.1 %copy-start.66 = (f32[16]{0:T(128)}, f32[16]{0:T(128)S(1)}, u32[]{:S(2)}) copy-start(f32[16]{0:T(128)S(1)} %reduce_sum.280) | copy-start | bytes 196
  123.5 93.9 %copy-start.76 = (f32[16]{0:T(128)}, f32[16]{0:T(128)S(1)}, u32[]{:S(2)}) copy-start(f32[16]{0:T(128)S(1)} %add_rsqrt_fusion.7) | copy-start | bytes 196
  213.7 22.2 %copy-start.2 = (bf16[8192,256]{1,0:T(8,128)(2,1)S(1)}, bf16[8192,256]{1,0:T(8,128)(2,1)}, u32[]{:S(2)}) copy-start(bf16[8192,256]{1,0:T(8,128)(2,1)} %all-gather.12.cloned.1.call-done) | copy-start | bytes 12582916
  218.2 29.4 %copy-start.71 = (f32[16]{0:T(128)}, f32[16]{0:T(128)S(1)}, u32[]{:S(2)}) copy-start(f32[16]{0:T(128)S(1)} %get-tuple-element.37) | copy-start | bytes 196
  227.9 16.7 %copy-start.54 = (f32[16]{0:T(128)}, f32[16]{0:T(128)S(1)}, u32[]{:S(2)}) copy-start(f32[16]{0:T(128)S(1)} %get-tuple-element.33) | copy-start | bytes 196
  234.2 9.4 %copy-start.56 = (f32[16]{0:T(128)}, f32[16]{0:T(128)S(1)}, u32[]{:S(2)}) copy-start(f32[16]{0:T(128)S(1)} %get-tuple-element.31) | copy-start | bytes 196
  242.4 11.7 %copy-start.65 = (s32[4,32]{1,0:T(4,128)S(1)}, s32[4,32]{1,0:T(4,128)}, u32[]{:S(2)}) copy-start(s32[4,32]{1,0:T(4,128)} %param.12) | copy-start | bytes 1540
  242.4 11.7 %copy-start.79 = (s32[4]{0:T(128)S(1)}, s32[4]{0:T(128)}, u32[]{:S(2)}) copy-start(s32[4]{0:T(128)} %iota_multiply_fusion) | copy-start | bytes 52
  242.4 11.7 %copy-start.78 = (s32[4,2]{0,1:T(2,128)S(1)}, s32[4,2]{0,1:T(2,128)}, u32[]{:S(2)}) copy-start(s32[4,2]{0,1:T(2,128)} %param.13) | copy-start | bytes 100
  244.6 17.9 %copy-start.77 = (f32[16]{0:T(128)S(1)}, f32[16]{0:T(128)}, u32[]{:S(2)}) copy-start(f32[16]{0:T(128)} %copy-done.76) | copy-start | bytes 196
  244.6 18.1 %copy-start.67 = (f32[16]{0:T(128)S(1)}, f32[16]{0:T(128)}, u32[]{:S(2)}) copy-start(f32[16]{0:T(128)} %copy-done.66) | copy-start | bytes 196
  244.6 18.1 %copy-start.57 = (f32[16]{0:T(128)S(1)}, f32[16]{0:T(128)}, u32[]{:S(2)}) copy-start(f32[16]{0:T(128)} %copy-done.56) | copy-start | bytes 196
  244.6 18.1 %copy-start.68 = (f32[16,1]{0,1:T(1,128)S(1)}, f32[16,1]{0,1:T(1,128)}, u32[]{:S(2)}) copy-start(f32[16,1]{0,1:T(1,128)} %get-tuple-element.36) | copy-start | bytes 196
  244.6 18.1 %copy-start.69 = (f32[16,1]{0,1:T(1,128)S(1)}, f32[16,1]{0,1:T(1,128)}, u32[]{:S(2)}) copy-start(f32[16,1]{0,1:T(1,128)} %get-tuple-element.144) | copy-start | bytes 196
  244.6 18.1 %copy-start.70 = (f32[16,1]{0,1:T(1,128)S(1)}, f32[16,1]{0,1:T(1,128)}, u32[]{:S(2)}) copy-start(f32[16,1]{0,1:T(1,128)} %get-tuple-element.34) | copy-start | bytes 196
  244.6 18.1 %copy-start.73 = (f32[16,1]{0,1:T(1,128)S(1)}, f32[16,1]{0,1:T(1,128)}, u32[]{:S(2)}) copy-start(f32[16,1]{0,1:T(1,128)} %get-tuple-element.32) | copy-start | bytes 196
  244.6 18.1 %copy-start.74 = (f32[16,1]{0,1:T(1,128)S(1)}, f32[16,1]{0,1:T(1,128)}, u32[]{:S(2)}) copy-start(f32[16,1]{0,1:T(1,128)} %get-tuple-element.30) | copy-start | bytes 196
  244.6 18.1 %copy-start.75 = (f32[16,1]{0,1:T(1,128)S(1)}, f32[16,1]{0,1:T(1,128)}, u32[]{:S(2)}) copy-start(f32[16,1]{0,1:T(1,128)} %get-tuple-element.28) | copy-start | bytes 196
  244.7 18.0 %copy-start.55 = (f32[16]{0:T(128)S(1)}, f32[16]{0:T(128)}, u32[]{:S(2)}) copy-start(f32[16]{0:T(128)} %copy-done.54) | copy-start | bytes 196
  247.6 15.1 %copy-start.72 = (f32[16]{0:T(128)S(1)}, f32[16]{0:T(128)}, u32[]{:S(2)}) copy-start(f32[16]{0:T(128)} %copy-done.71) | copy-start | bytes 196
  315.2 3.2 copy-start.1
  316.6 7.0 %copy-start.6 = (bf16[512,256]{1,0:T(8,128)(2,1)}, bf16[512,256]{1,0:T(8,128)(2,1)S(1)}, u32[]{:S(2)}) copy-start(bf16[512,256]{1,0:T(8,128)(2,1)S(1)} %get-tuple-element.175) | copy-start | bytes 786436
  316.6 3.4 copy-start.25
  316.6 3.4 copy-start.43
  316.6 3.4 copy-start.63
  318.1 5.7 %copy-start.9 = (bf16[512,256]{1,0:T(8,128)(2,1)}, bf16[512,256]{1,0:T(8,128)(2,1)S(1)}, u32[]{:S(2)}) copy-start(bf16[512,256]{1,0:T(8,128)(2,1)S(1)} %get-tuple-element.179) | copy-start | bytes 786436
  319.6 4.4 copy-start.7
  320.2 3.9 copy-start.4
  321.4 3.5 copy-start.39
  321.4 3.6 copy-start.33
  321.4 3.6 copy-start.47
  322.1 3.6 copy-start.10
  322.1 3.3 copy-start.52
  325.4 17.3 %copy-start.12 = (bf16[512,256]{1,0:T(8,128)(2,1)}, bf16[512,256]{1,0:T(8,128)(2,1)S(1)}, u32[]{:S(2)}) copy-start(bf16[512,256]{1,0:T(8,128)(2,1)S(1)} %get-tuple-element.197) | copy-start | bytes 786436
  325.7 16.5 %copy-start.15 = (bf16[512,256]{1,0:T(8,128)(2,1)}, bf16[512,256]{1,0:T(8,128)(2,1)S(1)}, u32[]{:S(2)}) copy-start(bf16[512,256]{1,0:T(8,128)(2,1)S(1)} %get-tuple-element.193) | copy-start | bytes 786436
  326.0 15.7 %copy-start.17 = (bf16[512,256]{1,0:T(8,128)(2,1)}, bf16[512,256]{1,0:T(8,128)(2,1)S(1)}, u32[]{:S(2)}) copy-start(bf16[512,256]{1,0:T(8,128)(2,1)S(1)} %get-tuple-element.189) | copy-start | bytes 786436
  326.3 14.8 %copy-start.19 = (bf16[512,256]{1,0:T(8,128)(2,1)}, bf16[512,256]{1,0:T(8,128)(2,1)S(1)}, u32[]{:S(2)}) copy-start(bf16[512,256]{1,0:T(8,128)(2,1)S(1)} %get-tuple-element.185) | copy-start | bytes 786436
  326.7 14.0 %copy-start.20 = (bf16[512,256]{1,0:T(8,128)(2,1)}, bf16[512,256]{1,0:T(8,128)(2,1)S(1)}, u32[]{:S(2)}) copy-start(bf16[512,256]{1,0:T(8,128)(2,1)S(1)} %get-tuple-element.181) | copy-start | bytes 786436
  327.3 12.9 %copy-start.21 = (bf16[512,256]{1,0:T(8,128)(2,1)}, bf16[512,256]{1,0:T(8,128)(2,1)S(1)}, u32[]{:S(2)}) copy-start(bf16[512,256]{1,0:T(8,128)(2,1)S(1)} %get-tuple-element.177) | copy-start | bytes 786436
  327.6 12.1 %copy-start.14 = (bf16[512,256]{1,0:T(8,128)(2,1)}, bf16[512,256]{1,0:T(8,128)(2,1)S(1)}, u32[]{:S(2)}) copy-start(bf16[512,256]{1,0:T(8,128)(2,1)S(1)} %fusion.14) | copy-start | bytes 786436
  327.6 3.4 copy-start.60
  327.9 3.6 copy-start.38
  331.6 3.4 copy-start.59
  331.9 3.6 copy-start.37
  335.6 3.4 copy-start.58
  336.0 3.6 copy-start.36
  339.7 3.4 copy-start.53
  386.2 9.8 %copy-start.8 = (bf16[512,256]{1,0:T(8,128)(2,1)S(1)}, bf16[512,256]{1,0:T(8,128)(2,1)}, u32[]{:S(2)}) copy-start(bf16[512,256]{1,0:T(8,128)(2,1)} %copy-done.7) | copy-start | bytes 786436
  387.5 9.5 %copy-start.18 = (bf16[512,256]{1,0:T(8,128)(2,1)S(1)}, bf16[512,256]{1,0:T(8,128)(2,1)}, u32[]{:S(2)}) copy-start(bf16[512,256]{1,0:T(8,128)(2,1)} %copy-done.17) | copy-start | bytes 786436
  389.5 7.9 %copy-start.5 = (bf16[512,256]{1,0:T(8,128)(2,1)S(1)}, bf16[512,256]{1,0:T(8,128)(2,1)}, u32[]{:S(2)}) copy-start(bf16[512,256]{1,0:T(8,128)(2,1)} %copy-done.4) | copy-start | bytes 786436
  390.8 7.5 %copy-start.16 = (bf16[512,256]{1,0:T(8,128)(2,1)S(1)}, bf16[512,256]{1,0:T(8,128)(2,1)}, u32[]{:S(2)}) copy-start(bf16[512,256]{1,0:T(8,128)(2,1)} %copy-done.15) | copy-start | bytes 786436
  394.0 5.6 %copy-start.13 = (bf16[512,256]{1,0:T(8,128)(2,1)S(1)}, bf16[512,256]{1,0:T(8,128)(2,1)}, u32[]{:S(2)}) copy-start(bf16[512,256]{1,0:T(8,128)(2,1)} %copy-done.12) | copy-start | bytes 786436
  397.3 4.0 copy-start.11
  402.3 33.2 %all-to-all-start.4 = ((bf16[8,256,256]{1,2,0:T(8,128)(2,1)}), bf16[8,256,256]{1,2,0:T(8,128)(2,1)S(1)}, u32[]{:S(2)}, u32[]{:S(2)}) async-start(bf16[8,256,256]{1,2,0:T(8,128)(2,1)} %fusion.217), calls=%async_computation.4 | async-start | bytes 2097152 | tf_op jit(solution)/shard_map/all_to_all | solution.py:153
  435.7 24.4 %collective-permute-start.1 = (f32[256,256]{0,1:T(8,128)S(1)}, f32[256,256]{0,1:T(8,128)S(1)}, u32[]{:S(2)}, u32[]{:S(2)}) collective-permute-start(f32[256,256]{0,1:T(8,128)S(1)} %convert_reduce_fusion.1), channel_id=1, source_target_pairs={{0,0},{4,32},{8,64},{12,96},{16,128},{20,160},{24,192},{28,224},{3... | collective-permute-start | bytes 786440 | tf_op jit(solution)/shard_map/ppermute | solution.py:154
  (26 other events, 41.6 us)
Sparse Core Ops, SparseCore 0:
  28.5 33.5 all-gather.9
  96.3 117.3 all-gather.11
  254.2 46.5 all-gather.7
